TPU v7x, 32 devices: a whole 2x2x4 slice. The times are simulated.
32 devices in a mesh: dp: 16 (over z, x, core), tensor: 2 (over y).
Axes of the slice: x: 2, y: 2, z: 4, core: 2. Of those that a mesh axis runs over, the one named last changes fastest.
Arguments:
- tokens: bfloat16 [4096, 2048], P(('dp', 'tensor')), may hold values from -6 to 6
- segment_ids: int32 [16, 256], P('dp'), may hold values from 0 to 3, never falling along the last dimension, each value on 1 to 128 neighbouring positions
- w_query: bfloat16 [2048, 2048], P('dp', 'tensor'), may hold values from -0.125 to 0.125
- w_key: bfloat16 [2048, 2048], P('dp', 'tensor'), may hold values from -0.125 to 0.125
- w_value: bfloat16 [2048, 2048], P('dp', 'tensor'), may hold values from -0.125 to 0.125
- w_output: bfloat16 [2048, 2048], P('dp', 'tensor'), may hold values from -0.125 to 0.125
- w_gate: bfloat16 [2048, 8192], P('dp', 'tensor'), may hold values from -0.125 to 0.125
- w_up: bfloat16 [2048, 8192], P('dp', 'tensor'), may hold values from -0.125 to 0.125
- w_down: bfloat16 [2048, 8192], P('dp', 'tensor'), may hold values from -0.0625 to 0.0625
- query_gain: float32 [2048], P(('dp', 'tensor')), may hold values from 0.5 to 2
- key_gain: float32 [2048], P(('dp', 'tensor')), may hold values from 0.5 to 2
- attn_gain: float32 [2048], P(('dp', 'tensor')), may hold values from 0.1 to 1.9
- ffn_gain: float32 [2048], P(('dp', 'tensor')), may hold values from 0.1 to 1.9
- cotangent: bfloat16 [4096, 2048], P(('dp', 'tensor')), may hold values from -6 to 6
Outputs:
- output: bfloat16 [4096, 2048], P(('dp', 'tensor'))
- grad_tokens: float32 [4096, 2048], P(('dp', 'tensor'))
- grad_query: float32 [2048, 2048], P('dp', 'tensor')
- grad_key: float32 [2048, 2048], P('dp', 'tensor')
- grad_value: float32 [2048, 2048], P('dp', 'tensor')
- grad_output: float32 [2048, 2048], P('dp', 'tensor')
- grad_gate: float32 [2048, 8192], P('dp', 'tensor')
- grad_up: float32 [2048, 8192], P('dp', 'tensor')
- grad_down: float32 [2048, 8192], P('dp', 'tensor')
- grad_query_gain: float32 [2048], P(('dp', 'tensor'))
- grad_key_gain: float32 [2048], P(('dp', 'tensor'))
- grad_attn_gain: float32 [2048], P(('dp', 'tensor'))
- grad_ffn_gain: float32 [2048], P(('dp', 'tensor'))
Inputs may be any that keep to these rules, and one draw needn't show every extreme that they name: `segment_ids`: within each sequence the ids never fall; each document has 1 to 128 tokens, and one has exactly 128.
All inputs are finite; a program needn't handle non-finite values.
Results may differ from a plain program's by a relative error of at most 0.015.
Values may be sent and summed in bfloat16 or wider, within the bound.
No kernel may reach another device: no remote copies, remote signals or barrier semaphores. Data moves between devices by JAX's collectives and lax.ppermute only.
A program may use at most 384 MiB of HBM per device.

v0:
```python
import math
import jax
import jax.numpy as jnp
from jax import lax
from jax.sharding import PartitionSpec as P

HD = 128
EPSILON = 1e-06
NEGATIVE = -1e30


def rms_scale(values):
    return lax.rsqrt(jnp.mean(values * values, axis=1, keepdims=True) + EPSILON)


def whole_rows(halves):
    return lax.all_gather(halves, "tensor", axis=0, tiled=True)


def to_halves(partial_value):
    return lax.psum_scatter(partial_value, "tensor", scatter_dimension=0, tiled=True)


def norm_totals(pair):
    return lax.psum((pair[0], pair[1]), "tensor")


def shards(
    tokens,
    segment_ids,
    w_query,
    w_key,
    w_value,
    w_output,
    w_gate,
    w_up,
    w_down,
    query_gain,
    key_gain,
    attn_gain,
    ffn_gain,
    cotangent,
):
    tensor_index = lax.axis_index("tensor")
    head_width = w_query.shape[1]
    ffn_width = w_gate.shape[1]
    own_rows = w_query.shape[0]
    model_width = own_rows * lax.axis_size("dp")
    seq_length = tokens.shape[0] * lax.axis_size("tensor")
    local_heads = head_width // HD
    score_scale = 1.0 / math.sqrt(HD)
    gains = lax.all_gather(
        jnp.stack([query_gain, key_gain, attn_gain, ffn_gain]), ("dp", "tensor"), axis=1, tiled=True
    )
    query_scale = lax.dynamic_slice_in_dim(gains[0], tensor_index * head_width, head_width)
    key_scale = lax.dynamic_slice_in_dim(gains[1], tensor_index * head_width, head_width)
    attn_scale = gains[2]
    ffn_scale = gains[3]
    positions = jnp.arange(seq_length)
    seq_ids = segment_ids[0]
    visible = (positions[:, None] >= positions[None, :]) & (seq_ids[:, None] == seq_ids[None, :])
    whole_input = whole_rows(tokens)
    pieces = (
        lax.all_gather(w_query, "dp", axis=0, tiled=True),
        lax.all_gather(w_key, "dp", axis=0, tiled=True),
        lax.all_gather(w_value, "dp", axis=0, tiled=True),
        lax.all_gather(w_output, "dp", axis=0, tiled=True),
    )
    columns = whole_input
    query_acc = jnp.dot(columns, pieces[0], preferred_element_type=jnp.float32)
    key_acc = jnp.dot(columns, pieces[1], preferred_element_type=jnp.float32)
    value_acc = jnp.dot(columns, pieces[2], preferred_element_type=jnp.float32)
    stored = pieces[3]
    query, key_proj, value_acc, output_rows = (query_acc, key_acc, value_acc, stored)
    squares = norm_totals((jnp.sum(query * query, axis=1), jnp.sum(key_proj * key_proj, axis=1)))
    q_rms = lax.rsqrt(squares[0] / model_width + EPSILON)[:, None]
    k_rms = lax.rsqrt(squares[1] / model_width + EPSILON)[:, None]
    normed_query = (query * q_rms * query_scale).astype(jnp.bfloat16)
    normed_key = (key_proj * k_rms * key_scale).astype(jnp.bfloat16)
    value_bf = value_acc.astype(jnp.bfloat16)
    query_heads = normed_query.reshape(seq_length, local_heads, HD)
    key_heads = normed_key.reshape(seq_length, local_heads, HD)
    value_heads = value_bf.reshape(seq_length, local_heads, HD)
    scores = (
        jnp.einsum("qhd,khd->hqk", query_heads, key_heads, preferred_element_type=jnp.float32)
        * score_scale
    )
    scores = jnp.where(visible[None], scores, NEGATIVE)
    peak = jnp.max(scores, axis=-1, keepdims=True)
    expo = jnp.exp(scores - peak)
    total = jnp.sum(expo, axis=-1, keepdims=True)
    log_total = peak + jnp.log(total)
    prob_bf = (expo / total).astype(jnp.bfloat16)
    attn_heads = jnp.einsum(
        "hqk,khd->qhd", prob_bf, value_heads, preferred_element_type=jnp.float32
    ).astype(jnp.bfloat16)
    attn = attn_heads.reshape(seq_length, head_width)
    proj = to_halves(jnp.einsum("sc,oc->so", attn, output_rows, preferred_element_type=jnp.float32))
    attn_rms = rms_scale(proj)
    resid = tokens.astype(jnp.float32) + proj * attn_rms * attn_scale
    whole_hidden = whole_rows(resid.astype(jnp.bfloat16))
    pieces = (
        lax.all_gather(w_gate, "dp", axis=0, tiled=True),
        lax.all_gather(w_up, "dp", axis=0, tiled=True),
        lax.all_gather(w_down, "dp", axis=0, tiled=True),
    )
    columns = whole_hidden
    gate_acc = jnp.dot(columns, pieces[0], preferred_element_type=jnp.float32)
    up_acc = jnp.dot(columns, pieces[1], preferred_element_type=jnp.float32)
    stored = pieces[2]
    sigma = jax.nn.sigmoid(gate_acc)
    act = (gate_acc * sigma * up_acc).astype(jnp.bfloat16)
    ffn = to_halves(jnp.einsum("sf,of->so", act, stored, preferred_element_type=jnp.float32))
    ffn_rms = rms_scale(ffn)
    output = (resid + ffn * ffn_rms * ffn_scale).astype(jnp.bfloat16)
    d_out = cotangent.astype(jnp.float32)
    ffn_gain_term = jnp.sum(d_out * ffn * ffn_rms, axis=0)
    scaled_out = d_out * ffn_scale
    d_ffn = (
        ffn_rms
        * (scaled_out - ffn * ffn_rms * ffn_rms * jnp.mean(scaled_out * ffn, axis=1, keepdims=True))
    ).astype(jnp.bfloat16)
    whole_dffn = whole_rows(d_ffn)
    d_act = jnp.dot(whole_dffn, stored, preferred_element_type=jnp.float32)
    d_gate = (d_act * up_acc * sigma * (1.0 + gate_acc * (1.0 - sigma))).astype(jnp.bfloat16)
    d_up = (d_act * gate_acc * sigma).astype(jnp.bfloat16)
    pieces = (
        lax.all_gather(w_gate, "dp", axis=0, tiled=True),
        lax.all_gather(w_up, "dp", axis=0, tiled=True),
    )
    block = jnp.einsum(
        "sf,rf->sr", d_gate, pieces[0], preferred_element_type=jnp.float32
    ) + jnp.einsum("sf,rf->sr", d_up, pieces[1], preferred_element_type=jnp.float32)
    hidden_part = block
    d_resid = d_out + to_halves(hidden_part)
    attn_gain_term = jnp.sum(d_resid * proj * attn_rms, axis=0)
    scaled_resid = d_resid * attn_scale
    d_proj = (
        attn_rms
        * (
            scaled_resid
            - proj * attn_rms * attn_rms * jnp.mean(scaled_resid * proj, axis=1, keepdims=True)
        )
    ).astype(jnp.bfloat16)
    whole_dproj = whole_rows(d_proj)
    d_attn = jnp.dot(whole_dproj, output_rows, preferred_element_type=jnp.float32).astype(
        jnp.bfloat16
    )
    d_attn_heads = d_attn.reshape(seq_length, local_heads, HD)
    back_prob = jnp.where(visible[None], jnp.exp(scores - log_total), 0.0)
    back_bf = back_prob.astype(jnp.bfloat16)
    d_value = (
        jnp.einsum("hqk,qhd->khd", back_bf, d_attn_heads, preferred_element_type=jnp.float32)
        .reshape(seq_length, head_width)
        .astype(jnp.bfloat16)
    )
    d_prob = jnp.einsum(
        "qhd,khd->hqk", d_attn_heads, value_heads, preferred_element_type=jnp.float32
    )
    delta = jnp.einsum("qhd,qhd->hq", d_attn_heads, attn_heads, preferred_element_type=jnp.float32)[
        ..., None
    ]
    d_score = (back_prob * (d_prob - delta)).astype(jnp.bfloat16)
    d_nq = (
        jnp.einsum("hqk,khd->qhd", d_score, key_heads, preferred_element_type=jnp.float32).reshape(
            seq_length, head_width
        )
        * score_scale
    )
    d_nk = (
        jnp.einsum(
            "hqk,qhd->khd", d_score, query_heads, preferred_element_type=jnp.float32
        ).reshape(seq_length, head_width)
        * score_scale
    )
    query_gain_term = jnp.sum(d_nq * query * q_rms, axis=0)
    key_gain_term = jnp.sum(d_nk * key_proj * k_rms, axis=0)
    scaled_q = d_nq * query_scale
    scaled_k = d_nk * key_scale
    inner = norm_totals((jnp.sum(scaled_q * query, axis=1), jnp.sum(scaled_k * key_proj, axis=1)))
    d_query = (
        q_rms * (scaled_q - query * q_rms * q_rms * (inner[0] / model_width)[:, None])
    ).astype(jnp.bfloat16)
    d_key = (
        k_rms * (scaled_k - key_proj * k_rms * k_rms * (inner[1] / model_width)[:, None])
    ).astype(jnp.bfloat16)
    pieces = (
        lax.all_gather(w_query, "dp", axis=0, tiled=True),
        lax.all_gather(w_key, "dp", axis=0, tiled=True),
        lax.all_gather(w_value, "dp", axis=0, tiled=True),
    )
    block = (
        jnp.einsum("sc,rc->sr", d_query, pieces[0], preferred_element_type=jnp.float32)
        + jnp.einsum("sc,rc->sr", d_key, pieces[1], preferred_element_type=jnp.float32)
        + jnp.einsum("sc,rc->sr", d_value, pieces[2], preferred_element_type=jnp.float32)
    )
    grad_tokens = d_resid + to_halves(block)
    gate_term = jnp.einsum("sr,sf->rf", whole_hidden, d_gate, preferred_element_type=jnp.float32)
    up_term = jnp.einsum("sr,sf->rf", whole_hidden, d_up, preferred_element_type=jnp.float32)
    down_term = jnp.einsum("sr,sf->rf", whole_dffn, act, preferred_element_type=jnp.float32)
    query_term = jnp.einsum("sr,sc->rc", whole_input, d_query, preferred_element_type=jnp.float32)
    key_term = jnp.einsum("sr,sc->rc", whole_input, d_key, preferred_element_type=jnp.float32)
    value_term = jnp.einsum("sr,sc->rc", whole_input, d_value, preferred_element_type=jnp.float32)
    output_term = jnp.einsum("sr,sc->rc", whole_dproj, attn, preferred_element_type=jnp.float32)
    combined = lax.psum_scatter(
        jnp.concatenate(
            [
                jnp.concatenate([query_term, key_term, value_term, output_term], axis=1),
                jnp.concatenate([gate_term, up_term, down_term], axis=1),
            ],
            axis=1,
        ),
        "dp",
        scatter_dimension=0,
        tiled=True,
    )
    attn_sums = combined[:, : 4 * head_width]
    mlp_sums = combined[:, 4 * head_width :]
    gain_zero = jnp.zeros((model_width,), jnp.float32)
    query_placed = lax.dynamic_update_slice_in_dim(
        gain_zero, query_gain_term, tensor_index * head_width, 0
    )
    key_placed = lax.dynamic_update_slice_in_dim(
        gain_zero, key_gain_term, tensor_index * head_width, 0
    )
    gain_parts = lax.psum_scatter(
        jnp.stack([query_placed, key_placed, attn_gain_term, ffn_gain_term]),
        ("dp", "tensor"),
        scatter_dimension=1,
        tiled=True,
    )
    grad_query = attn_sums[:, :head_width]
    grad_key = attn_sums[:, head_width : 2 * head_width]
    grad_value = attn_sums[:, 2 * head_width : 3 * head_width]
    grad_output = attn_sums[:, 3 * head_width :]
    grad_gate = mlp_sums[:, :ffn_width]
    grad_up = mlp_sums[:, ffn_width : 2 * ffn_width]
    grad_down = mlp_sums[:, 2 * ffn_width :]
    return (
        output,
        grad_tokens,
        grad_query,
        grad_key,
        grad_value,
        grad_output,
        grad_gate,
        grad_up,
        grad_down,
        gain_parts[0],
        gain_parts[1],
        gain_parts[2],
        gain_parts[3],
    )


def solution(mesh):
    return jax.shard_map(
        shards,
        mesh=mesh,
        in_specs=(
            P(("dp", "tensor"), None),
            P("dp", None),
            P("dp", "tensor"),
            P("dp", "tensor"),
            P("dp", "tensor"),
            P("dp", "tensor"),
            P("dp", "tensor"),
            P("dp", "tensor"),
            P("dp", "tensor"),
            P(("dp", "tensor")),
            P(("dp", "tensor")),
            P(("dp", "tensor")),
            P(("dp", "tensor")),
            P(("dp", "tensor"), None),
        ),
        out_specs=(
            P(("dp", "tensor"), None),
            P(("dp", "tensor"), None),
            P("dp", "tensor"),
            P("dp", "tensor"),
            P("dp", "tensor"),
            P("dp", "tensor"),
            P("dp", "tensor"),
            P("dp", "tensor"),
            P("dp", "tensor"),
            P(("dp", "tensor")),
            P(("dp", "tensor")),
            P(("dp", "tensor")),
            P(("dp", "tensor")),
        ),
        check_vma=False,
    )
```

profile of v0, /device:TPU:0, one launch (start us, length us, event | category | flops | bytes accessed | tf_op | source)
XLA Modules:
  0.0 2323.6 jit_solution(9547360384983591995)
XLA Ops:
  11.3 71.0 %all-gather = f32[32,64,4]{1,2,0:T(4,128)S(1)} all-gather(f32[1,64,4]{1,2,0:T(4,128)S(1)} %maximum_bitcast_fusion), channel_id=1, replica_groups=mesh['dp'=16,'tensor'=2] {'dp','tensor'}, dimensions={0}, use_global_device_ids=true | all-gather | bytes 33792 | tf_op jit(solution)/shard_map/all_gather | solution.py:52
  90.3 47.3 %all-gather.19.cloned.1.call-done = bf16[2048,1024]{1,0:T(8,128)(2,1)} async-done(((bf16[128,1024]{1,0:T(8,128)(2,1)}), bf16[2048,1024]{1,0:T(8,128)(2,1)}) %all-gather.19.cloned.1.call-update) | async-done | bytes 4194320 | tf_op jit(solution)/shard_map/all_gather | solution.py:65
  141.2 4.9 all-reduce.1
  152.3 36.3 %all-gather.15.cloned.1.call-done = bf16[2048,1024]{1,0:T(8,128)(2,1)} async-done(((bf16[128,1024]{1,0:T(8,128)(2,1)}), bf16[2048,1024]{1,0:T(8,128)(2,1)}) %all-gather.15.cloned.1.call-update) | async-done | bytes 4194320 | tf_op jit(solution)/shard_map/all_gather | solution.py:66
  193.4 46.1 %all-gather.21.cloned.1.call-done = bf16[2048,1024]{1,0:T(8,128)(2,1)} async-done(((bf16[128,1024]{1,0:T(8,128)(2,1)}), bf16[2048,1024]{1,0:T(8,128)(2,1)}) %all-gather.21.cloned.1.call-update) | async-done | bytes 4194320 | tf_op jit(solution)/shard_map/all_gather | solution.py:67
  244.5 30.5 %reduce-scatter.9.cloned.1.call-done = f32[128,2048]{1,0:T(8,128)} async-done(((f32[256,2048]{1,0:T(8,128)}), f32[128,2048]{1,0:T(8,128)}) %reduce-scatter.9.cloned.1.call-update) | async-done | bytes 1048592 | tf_op jit(solution)/shard_map/reduce_scatter | solution.py:21
  281.0 19.1 all-gather.23.cloned.1.call-done
  300.1 128.6 %all-gather.25.cloned.1.call-done = bf16[2048,4096]{1,0:T(8,128)(2,1)} async-done(((bf16[128,4096]{1,0:T(8,128)(2,1)}), bf16[2048,4096]{1,0:T(8,128)(2,1)}) %all-gather.25.cloned.1.call-update) | async-done | bytes 16777232 | tf_op jit(solution)/shard_map/all_gather | solution.py:103
  428.8 12.6 fusion.29
  441.3 114.2 %all-gather.27.cloned.1.call-done = bf16[2048,4096]{1,0:T(8,128)(2,1)} async-done(((bf16[128,4096]{1,0:T(8,128)(2,1)}), bf16[2048,4096]{1,0:T(8,128)(2,1)}) %all-gather.27.cloned.1.call-update) | async-done | bytes 16777232 | tf_op jit(solution)/shard_map/all_gather | solution.py:104
  555.6 13.4 multiply_convert_fusion.2
  569.0 113.2 %all-gather.29.cloned.1.call-done = bf16[2048,4096]{1,0:T(8,128)(2,1)} async-done(((bf16[128,4096]{1,0:T(8,128)(2,1)}), bf16[2048,4096]{1,0:T(8,128)(2,1)}) %all-gather.29.cloned.1.call-update) | async-done | bytes 16777232 | tf_op jit(solution)/shard_map/all_gather | solution.py:105
  682.2 12.3 fusion.30
  694.6 30.2 %reduce-scatter.11.cloned.1.call-done = f32[128,2048]{1,0:T(8,128)} async-done(((f32[256,2048]{1,0:T(8,128)}), f32[128,2048]{1,0:T(8,128)}) %reduce-scatter.11.cloned.1.call-update) | async-done | bytes 1048592 | tf_op jit(solution)/shard_map/reduce_scatter | solution.py:21
  730.3 21.2 all-gather.31.cloned.1.call-done
  751.5 16.0 multiply_convert_fusion
  767.5 12.2 fusion.31
  779.7 13.3 convolution_add_fusion.2
  793.0 32.0 %reduce-scatter.13.cloned.1.call-done = f32[128,2048]{1,0:T(8,128)} async-done(((f32[256,2048]{1,0:T(8,128)}), f32[128,2048]{1,0:T(8,128)}) %reduce-scatter.13.cloned.1.call-update) | async-done | bytes 1048592 | tf_op jit(solution)/shard_map/reduce_scatter | solution.py:21
  830.2 21.4 all-gather.33.cloned.1.call-done
  887.1 9.4 copy.82
  914.6 8.3 constant_dynamic-update-slice_fusion.2
  922.9 9.3 copy.83
  932.2 9.3 copy.84
  941.8 8.5 constant_dynamic-update-slice_fusion.1
  959.2 13.3 convolution_dynamic-update-slice_fusion.2
  972.5 13.2 convolution_dynamic-update-slice_fusion.1
  985.7 13.2 convolution_dynamic-update-slice_fusion
  999.0 36.0 %reduce-scatter.19.cloned.1.call-done = f32[64,4]{1,0:T(8,128)} async-done(((f32[2048,4]{1,0:T(8,128)}), f32[64,4]{1,0:T(8,128)}) %reduce-scatter.19.cloned.1.call-update) | async-done | bytes 1040
  1038.3 26.8 %reduce-scatter.15.cloned.1.call-done = f32[128,2048]{1,0:T(8,128)} async-done(((f32[256,2048]{1,0:T(8,128)}), f32[128,2048]{1,0:T(8,128)}) %reduce-scatter.15.cloned.1.call-update) | async-done | bytes 1048592 | tf_op jit(solution)/shard_map/reduce_scatter | solution.py:21
  1067.4 1240.7 %reduce-scatter.17.cloned.1.call-done = f32[128,16384]{1,0:T(8,128)} async-done(((f32[2048,16384]{1,0:T(8,128)}), f32[128,16384]{1,0:T(8,128)}) %reduce-scatter.17.cloned.1.call-update) | async-done | bytes 8388624 | tf_op jit(solution)/shard_map/reduce_scatter | solution.py:205
  2311.1 5.8 fusion.23
  (173 shorter events, 119.3 us)
Async XLA Ops:
  7.2 76.2 %all-gather.13.cloned.1.call-start = ((), (), s32[]{:S(2)}) async-start(), calls=%async_computation.6 | async-start | bytes 1572864 | tf_op jit(solution)/shard_map/all_gather | solution.py:17
  7.9 78.5 %all-gather.17.cloned.1.call-start = ((), (), s32[]{:S(2)}) async-start(), calls=%async_computation.8 | async-start | bytes 4456448 | tf_op jit(solution)/shard_map/all_gather | solution.py:64
  8.7 129.0 %all-gather.19.cloned.1.call-start = ((), (), s32[]{:S(2)}) async-start(), calls=%async_computation.9 | async-start | bytes 4456448 | tf_op jit(solution)/shard_map/all_gather | solution.py:65
  9.4 179.2 %all-gather.15.cloned.1.call-start = ((), (), s32[]{:S(2)}) async-start(), calls=%async_computation.7 | async-start | bytes 4456448 | tf_op jit(solution)/shard_map/all_gather | solution.py:66
  10.0 229.6 %all-gather.21.cloned.1.call-start = ((), (), s32[]{:S(2)}) async-start(), calls=%async_computation.10 | async-start | bytes 4456448 | tf_op jit(solution)/shard_map/all_gather | solution.py:67
  10.6 264.5 %reduce-scatter.9.cloned.1.call-start = ((), (), s32[]{:S(2)}) async-start(), calls=%async_computation.11 | async-start | bytes 3145728 | tf_op jit(solution)/shard_map/reduce_scatter | solution.py:21
  83.4 54.2 %copy-start.4 = (bf16[256,2048]{1,0:T(8,128)(2,1)S(1)}, bf16[256,2048]{1,0:T(8,128)(2,1)}, u32[]{:S(2)}) copy-start(bf16[256,2048]{1,0:T(8,128)(2,1)} %all-gather.13.cloned.1.call-done) | copy-start | bytes 3145732
  90.3 56.8 %copy-start.8 = (f32[256,1024]{1,0:T(8,128)}, f32[256,1024]{1,0:T(8,128)S(1)}, u32[]{:S(2)}) copy-start(f32[256,1024]{1,0:T(8,128)S(1)} %get-tuple-element.45) | copy-start | bytes 3145732
  141.1 9.1 copy-start.6
  193.4 51.0 %copy-start.23 = (bf16[8,128,256]{2,1,0:T(8,128)(2,1)}, bf16[8,128,256]{2,1,0:T(8,128)(2,1)S(1)}, u32[]{:S(2)}) copy-start(bf16[8,128,256]{2,1,0:T(8,128)(2,1)S(1)} %convolution_convert_fusion.1) | copy-start | bytes 1572868
  239.5 36.9 %copy-start.15 = (bf16[128,2048]{1,0:T(8,128)(2,1)S(1)}, bf16[128,2048]{1,0:T(8,128)(2,1)}, u32[]{:S(2)}) copy-start(bf16[128,2048]{1,0:T(8,128)(2,1)} %param.14) | copy-start | bytes 1572868
  244.4 55.7 %all-gather.23.cloned.1.call-start = ((), (), s32[]{:S(2)}) async-start(), calls=%async_computation.12 | async-start | bytes 1572864 | tf_op jit(solution)/shard_map/all_gather | solution.py:17
  278.7 150.1 %all-gather.25.cloned.1.call-start = ((), (), s32[]{:S(2)}) async-start(), calls=%async_computation.13 | async-start | bytes 17825792 | tf_op jit(solution)/shard_map/all_gather | solution.py:103
  279.5 276.1 %all-gather.27.cloned.1.call-start = ((), (), s32[]{:S(2)}) async-start(), calls=%async_computation.14 | async-start | bytes 17825792 | tf_op jit(solution)/shard_map/all_gather | solution.py:104
  280.2 402.0 %all-gather.29.cloned.1.call-start = ((), (), s32[]{:S(2)}) async-start(), calls=%async_computation.15 | async-start | bytes 17825792 | tf_op jit(solution)/shard_map/all_gather | solution.py:105
  280.8 444.0 %reduce-scatter.11.cloned.1.call-start = ((), (), s32[]{:S(2)}) async-start(), calls=%async_computation.16 | async-start | bytes 3145728 | tf_op jit(solution)/shard_map/reduce_scatter | solution.py:21
  300.1 255.4 %copy-start.13 = (bf16[256,2048]{1,0:T(8,128)(2,1)S(1)}, bf16[256,2048]{1,0:T(8,128)(2,1)}, u32[]{:S(2)}) copy-start(bf16[256,2048]{1,0:T(8,128)(2,1)} %all-gather.23.cloned.1.call-done) | copy-start | bytes 3145732
  682.2 44.0 %copy-start.2 = (bf16[128,2048]{1,0:T(8,128)(2,1)S(1)}, bf16[128,2048]{1,0:T(8,128)(2,1)}, u32[]{:S(2)}) copy-start(bf16[128,2048]{1,0:T(8,128)(2,1)} %param.27) | copy-start | bytes 1572868
  694.5 57.0 %all-gather.31.cloned.1.call-start = ((), (), s32[]{:S(2)}) async-start(), calls=%async_computation.17 | async-start | bytes 1572864 | tf_op jit(solution)/shard_map/all_gather | solution.py:17
  730.1 94.9 %reduce-scatter.13.cloned.1.call-start = ((), (), s32[]{:S(2)}) async-start(), calls=%async_computation.18 | async-start | bytes 3145728 | tf_op jit(solution)/shard_map/reduce_scatter | solution.py:21
  779.7 45.3 %copy-start.1 = (f32[128,2048]{1,0:T(8,128)S(1)}, f32[128,2048]{1,0:T(8,128)}, u32[]{:S(2)}) copy-start(f32[128,2048]{1,0:T(8,128)} %reduce-scatter.9.cloned.1.call-done) | copy-start | bytes 3145732
  793.0 58.6 %all-gather.33.cloned.1.call-start = ((), (), s32[]{:S(2)}) async-start(), calls=%async_computation.19 | async-start | bytes 1572864 | tf_op jit(solution)/shard_map/all_gather | solution.py:17
  830.1 204.8 %reduce-scatter.19.cloned.1.call-start = ((), (), s32[]{:S(2)}) async-start(), calls=%async_computation.22 | async-start | bytes 1081344
  872.7 9.8 copy-start.5
  887.1 11.1 copy-start.28
  897.9 167.2 %reduce-scatter.15.cloned.1.call-start = ((), (), s32[]{:S(2)}) async-start(), calls=%async_computation.20 | async-start | bytes 3145728 | tf_op jit(solution)/shard_map/reduce_scatter | solution.py:21
  941.5 1366.6 %reduce-scatter.17.cloned.1.call-start = ((), (), s32[]{:S(2)}) async-start(), calls=%async_computation.21 | async-start | bytes 142606336 | tf_op jit(solution)/shard_map/reduce_scatter | solution.py:205
  959.1 13.3 copy-start.21
  972.5 13.2 copy-start.20
  972.5 13.2 copy-start.30
  999.0 66.1 %copy-start.3 = (bf16[128,2048]{1,0:T(8,128)(2,1)S(1)}, bf16[128,2048]{1,0:T(8,128)(2,1)}, u32[]{:S(2)}) copy-start(bf16[128,2048]{1,0:T(8,128)(2,1)} %param.27) | copy-start | bytes 1572868
  999.0 66.1 %copy-start.10 = (f32[128,2048]{1,0:T(8,128)S(1)}, f32[128,2048]{1,0:T(8,128)}, u32[]{:S(2)}) copy-start(f32[128,2048]{1,0:T(8,128)} %reduce-scatter.13.cloned.1.call-done) | copy-start | bytes 3145732
  (17 other events, 73.1 us)
Sparse Core Ops, SparseCore 0:
  9.5 24.2 all-gather.12
  36.0 50.3 all-gather.16
  88.6 48.9 all-gather.18
  139.6 48.8 all-gather.14
  190.6 48.8 all-gather.20
  244.6 30.4 reduce-scatter.8
  278.8 21.2 all-gather.22
  302.3 126.4 all-gather.24
  430.9 124.5 all-gather.26
  557.6 124.5 all-gather.28
  694.7 30.0 reduce-scatter.10
  730.2 21.2 all-gather.30
  793.1 31.8 reduce-scatter.12
  830.2 21.2 all-gather.32
  898.0 136.8 reduce-scatter.18
  1037.0 27.9 reduce-scatter.14
  1069.2 1238.9 reduce-scatter.16
where the time goes:
time: 2330 us; the launch traced here: 2320 us
  waiting for transfers between devices  1950 us (84%)
  matrix products  173 us (7%)
  blocking collectives  80.9 us (3%)
  local copies, waits for them, and re-layouts  74.9 us (3%)
  other arithmetic  27.1 us (1%)
    reduce_scatter x1, waiting for transfers between devices, shards(): lax.psum_scatter(jnp.concatenate([jnp.concatenate([query_term, key_term,...  1240 us
    all_gather x1, waiting for transfers between devices, shards(): lax.all_gather(w_gate, 'dp', axis=0, tiled=True)  129 us
    reduce_scatter x4, waiting for transfers between devices, to_halves(): lax.psum_scatter(partial_value, 'tensor', scatter_dimension=0, tiled=True)  120 us
    all_gather x1, waiting for transfers between devices, shards(): lax.all_gather(w_up, 'dp', axis=0, tiled=True)  114 us
    all_gather x1, waiting for transfers between devices, shards(): lax.all_gather(w_down, 'dp', axis=0, tiled=True)  113 us
    all_gather x1, blocking collectives, shards(): lax.all_gather(jnp.stack([query_gain, key_gain, attn_gain, ffn_gain]), ('...  71 us
    all_gather x4, waiting for transfers between devices, whole_rows(): return lax.all_gather(halves, 'tensor', axis=0, tiled=True)  61.7 us
    all_gather x1, waiting for transfers between devices, shards(): lax.all_gather(w_key, 'dp', axis=0, tiled=True)  47.3 us
  transfers between devices with their start and end apart: 17, of which 16 were waited for; matrix products, arithmetic and copies ran while one was open for 7% of the time, Pallas kernels for 0%

commit v1 on v0

--- a/solution.py
+++ b/solution.py
@@ -7,6 +7,34 @@
 HD = 128
 EPSILON = 1e-06
 NEGATIVE = -1e30
+
+
+def values_register(sample, in_dim):
+    sample = jnp.moveaxis(sample, 0, in_dim)
+    local_part = sample.shape
+    return sample.reshape(
+        *local_part[:in_dim], local_part[in_dim] * local_part[in_dim + 1], *local_part[in_dim + 2 :]
+    )
+
+
+def advance_results(inputs, axis_key, along_dim):
+    n_parts = jax.lax.psum(1, axis_key)
+    block_list = tuple(((dev_i, (dev_i + 1) % n_parts) for dev_i in range(n_parts)))
+    seen = tuple(((idx, j0) for j0, idx in block_list))
+    reply, k_now = ([], [])
+    at = 0
+    while at < n_parts - 1:
+        if at % 2 == 0:
+            reply.append(jax.lax.ppermute(reply[-1] if reply else inputs, axis_key, block_list))
+        else:
+            h_now = jax.lax.ppermute(k_now[-1] if k_now else inputs, axis_key, seen)
+            k_now.append(h_now)
+        at = at + 1
+    taken_in = jnp.stack([*reply[::-1], inputs, *k_now], 0)
+    y = jax.lax.axis_index(axis_key)
+    known = y - len(reply)
+    taken_in = taken_in[(jnp.arange(n_parts) - known) % n_parts]
+    return values_register(taken_in, along_dim)
 
 
 def rms_scale(values):
@@ -100,7 +128,7 @@
     resid = tokens.astype(jnp.float32) + proj * attn_rms * attn_scale
     whole_hidden = whole_rows(resid.astype(jnp.bfloat16))
     pieces = (
-        lax.all_gather(w_gate, "dp", axis=0, tiled=True),
+        advance_results(w_gate, "dp", 0),
         lax.all_gather(w_up, "dp", axis=0, tiled=True),
         lax.all_gather(w_down, "dp", axis=0, tiled=True),
     )

time: 2330 us -> 2400 us (1.030)
  starting transfers between devices: 1.45 us -> 98.2 us
  waiting for transfers between devices: 1950 us -> 1880 us
  local copies, waits for them, and re-layouts: 74.9 us -> 112 us
    ppermute x0 -> x15, waiting for transfers between devices: none -> 137 us  [the longest x8 120 us: advance_results(): jax.lax.ppermute(reply[-1] if reply else inputs, axis_key, block_list)]
    all_gather x1, waiting for transfers between devices: 114 us -> 0.01 us  [shards(): lax.all_gather(w_up, 'dp', axis=0, tiled=True)]
    ppermute x0 -> x15, starting transfers between devices: none -> 96.6 us  [the longest x8 78.5 us: advance_results(): jax.lax.ppermute(reply[-1] if reply else inputs, axis_key, block_list)]
    all_gather x1, waiting for transfers between devices: 113 us -> 60.5 us  [shards(): lax.all_gather(w_down, 'dp', axis=0, tiled=True)]
    unnamed x75 -> x128, local copies, waits for them, and re-layouts: 28.4 us -> 51.5 us
  transfers between devices with their start and end apart: 17 -> 32, of which waited for: 16 -> 24; matrix products, arithmetic and copies ran while one was open for 7% -> 9% of each run, Pallas kernels for 0% -> 0%
where the time goes in v1:
time: 2400 us; the launch traced here: 2390 us
  waiting for transfers between devices  1880 us (78%)
  matrix products  174 us (7%)
  local copies, waits for them, and re-layouts  112 us (5%)
  starting transfers between devices  98.2 us (4%)
  blocking collectives  80.9 us (3%)
  other arithmetic  27.1 us (1%)
    reduce_scatter x1, waiting for transfers between devices, shards(): lax.psum_scatter(jnp.concatenate([jnp.concatenate([query_term, key_term,...  1240 us
    ppermute x8, waiting for transfers between devices, advance_results(): jax.lax.ppermute(reply[-1] if reply else inputs, axis_key, block_list)  120 us
    reduce_scatter x4, waiting for transfers between devices, to_halves(): lax.psum_scatter(partial_value, 'tensor', scatter_dimension=0, tiled=True)  118 us
    all_gather x1, waiting for transfers between devices, shards(): lax.all_gather(w_gate, 'dp', axis=0, tiled=True)  113 us
    ppermute x8, starting transfers between devices, advance_results(): jax.lax.ppermute(reply[-1] if reply else inputs, axis_key, block_list)  78.5 us
    all_gather x1, blocking collectives, shards(): lax.all_gather(jnp.stack([query_gain, key_gain, attn_gain, ffn_gain]), ('...  71 us
    all_gather x1, waiting for transfers between devices, shards(): lax.all_gather(w_down, 'dp', axis=0, tiled=True)  60.5 us
    unnamed x128, local copies, waits for them, and re-layouts  51.5 us
  transfers between devices with their start and end apart: 32, of which 24 were waited for; matrix products, arithmetic and copies ran while one was open for 9% of the time, Pallas kernels for 0%

profile of v1, /device:TPU:0, one launch (start us, length us, event | category | flops | bytes accessed | tf_op | source)
XLA Modules:
  0.0 2389.5 jit_solution(10581452859004658294)
XLA Ops:
  11.3 71.0 %all-gather = f32[32,64,4]{1,2,0:T(4,128)S(1)} all-gather(f32[1,64,4]{1,2,0:T(4,128)S(1)} %maximum_bitcast_fusion), channel_id=1, replica_groups=mesh['dp'=16,'tensor'=2] {'dp','tensor'}, dimensions={0}, use_global_device_ids=true | all-gather | bytes 33792 | tf_op jit(solution)/shard_map/all_gather | solution.py:80
  90.3 47.3 %all-gather.19.cloned.1.call-done = bf16[2048,1024]{1,0:T(8,128)(2,1)} async-done(((bf16[128,1024]{1,0:T(8,128)(2,1)}), bf16[2048,1024]{1,0:T(8,128)(2,1)}) %all-gather.19.cloned.1.call-update) | async-done | bytes 4194320 | tf_op jit(solution)/shard_map/all_gather | solution.py:93
  152.3 36.3 %all-gather.15.cloned.1.call-done = bf16[2048,1024]{1,0:T(8,128)(2,1)} async-done(((bf16[128,1024]{1,0:T(8,128)(2,1)}), bf16[2048,1024]{1,0:T(8,128)(2,1)}) %all-gather.15.cloned.1.call-update) | async-done | bytes 4194320 | tf_op jit(solution)/shard_map/all_gather | solution.py:94
  193.4 46.1 %all-gather.21.cloned.1.call-done = bf16[2048,1024]{1,0:T(8,128)(2,1)} async-done(((bf16[128,1024]{1,0:T(8,128)(2,1)}), bf16[2048,1024]{1,0:T(8,128)(2,1)}) %all-gather.21.cloned.1.call-update) | async-done | bytes 4194320 | tf_op jit(solution)/shard_map/all_gather | solution.py:95
  244.5 30.5 %reduce-scatter.9.cloned.1.call-done = f32[128,2048]{1,0:T(8,128)} async-done(((f32[256,2048]{1,0:T(8,128)}), f32[128,2048]{1,0:T(8,128)}) %reduce-scatter.9.cloned.1.call-update) | async-done | bytes 1048592 | tf_op jit(solution)/shard_map/reduce_scatter | solution.py:49
  280.3 17.1 collective-permute-done
  301.9 12.6 collective-permute-done.1
  314.5 16.1 collective-permute-start.2
  331.5 22.5 collective-permute-done.2
  401.0 14.5 collective-permute-done.4
  415.5 22.4 collective-permute-start.5
  440.2 30.5 %collective-permute-start.6 = (bf16[128,4096]{1,0:T(8,128)(2,1)S(1)}, bf16[128,4096]{1,0:T(8,128)(2,1)}, u32[]{:S(2)}, u32[]{:S(2)}) collective-permute-start(bf16[128,4096]{1,0:T(8,128)(2,1)S(1)} %collective-permute-done.5), channel_id=1, source_target_pairs={{0,2},{2,4},{4,6},{6,8},{8,10},{10,12},{12,14},{14,16},{16,18},{18... | collective-permute-start | bytes 3145736 | tf_op jit(solution)/shard_map/ppermute | solution.py:28
  470.8 27.7 %collective-permute-done.6 = bf16[128,4096]{1,0:T(8,128)(2,1)} collective-permute-done((bf16[128,4096]{1,0:T(8,128)(2,1)S(1)}, bf16[128,4096]{1,0:T(8,128)(2,1)}, u32[]{:S(2)}, u32[]{:S(2)}) %collective-permute-start.6) | collective-permute-done | bytes 1048608 | tf_op jit(solution)/shard_map/ppermute | solution.py:28
  503.0 12.8 collective-permute-done.7
  537.9 13.4 gather_fusion
  551.3 12.7 fusion.31
  564.0 14.9 multiply_convert_fusion.2
  578.9 60.5 %all-gather.27.cloned.1.call-done = bf16[2048,4096]{1,0:T(8,128)(2,1)} async-done(((bf16[128,4096]{1,0:T(8,128)(2,1)}), bf16[2048,4096]{1,0:T(8,128)(2,1)}) %all-gather.27.cloned.1.call-update) | async-done | bytes 16777232 | tf_op jit(solution)/shard_map/all_gather | solution.py:133
  639.4 12.3 fusion.32
  651.8 30.2 %reduce-scatter.11.cloned.1.call-done = f32[128,2048]{1,0:T(8,128)} async-done(((f32[256,2048]{1,0:T(8,128)}), f32[128,2048]{1,0:T(8,128)}) %reduce-scatter.11.cloned.1.call-update) | async-done | bytes 1048592 | tf_op jit(solution)/shard_map/reduce_scatter | solution.py:49
  688.3 20.4 all-gather.29.cloned.1.call-done
  708.7 16.0 multiply_convert_fusion
  724.6 112.5 %all-gather.31.cloned.1.call-done = bf16[2048,4096]{1,0:T(8,128)(2,1)} async-done(((bf16[128,4096]{1,0:T(8,128)(2,1)}), bf16[2048,4096]{1,0:T(8,128)(2,1)}) %all-gather.31.cloned.1.call-update) | async-done | bytes 16777232 | tf_op jit(solution)/shard_map/all_gather | solution.py:156
  849.4 13.1 convolution_add_fusion.2
  862.6 30.2 %reduce-scatter.13.cloned.1.call-done = f32[128,2048]{1,0:T(8,128)} async-done(((f32[256,2048]{1,0:T(8,128)}), f32[128,2048]{1,0:T(8,128)}) %reduce-scatter.13.cloned.1.call-update) | async-done | bytes 1048592 | tf_op jit(solution)/shard_map/reduce_scatter | solution.py:49
  898.0 21.3 all-gather.33.cloned.1.call-done
  1026.9 13.3 convolution_dynamic-update-slice_fusion.2
  1040.3 13.2 convolution_dynamic-update-slice_fusion.1
  1053.5 13.3 convolution_dynamic-update-slice_fusion
  1066.9 35.4 %reduce-scatter.19.cloned.1.call-done = f32[64,4]{1,0:T(8,128)} async-done(((f32[2048,4]{1,0:T(8,128)}), f32[64,4]{1,0:T(8,128)}) %reduce-scatter.19.cloned.1.call-update) | async-done | bytes 1040
  1105.6 26.7 %reduce-scatter.15.cloned.1.call-done = f32[128,2048]{1,0:T(8,128)} async-done(((f32[256,2048]{1,0:T(8,128)}), f32[128,2048]{1,0:T(8,128)}) %reduce-scatter.15.cloned.1.call-update) | async-done | bytes 1048592 | tf_op jit(solution)/shard_map/reduce_scatter | solution.py:49
  1134.7 1239.2 %reduce-scatter.17.cloned.1.call-done = f32[128,16384]{1,0:T(8,128)} async-done(((f32[2048,16384]{1,0:T(8,128)}), f32[128,16384]{1,0:T(8,128)}) %reduce-scatter.17.cloned.1.call-update) | async-done | bytes 8388624 | tf_op jit(solution)/shard_map/reduce_scatter | solution.py:233
  (260 shorter events, 268.6 us)
Async XLA Ops:
  7.2 76.2 %all-gather.13.cloned.1.call-start = ((), (), s32[]{:S(2)}) async-start(), calls=%async_computation.6 | async-start | bytes 1572864 | tf_op jit(solution)/shard_map/all_gather | solution.py:45
  7.9 78.5 %all-gather.17.cloned.1.call-start = ((), (), s32[]{:S(2)}) async-start(), calls=%async_computation.8 | async-start | bytes 4456448 | tf_op jit(solution)/shard_map/all_gather | solution.py:92
  8.7 129.0 %all-gather.19.cloned.1.call-start = ((), (), s32[]{:S(2)}) async-start(), calls=%async_computation.9 | async-start | bytes 4456448 | tf_op jit(solution)/shard_map/all_gather | solution.py:93
  9.4 179.2 %all-gather.15.cloned.1.call-start = ((), (), s32[]{:S(2)}) async-start(), calls=%async_computation.7 | async-start | bytes 4456448 | tf_op jit(solution)/shard_map/all_gather | solution.py:94
  10.0 229.6 %all-gather.21.cloned.1.call-start = ((), (), s32[]{:S(2)}) async-start(), calls=%async_computation.10 | async-start | bytes 4456448 | tf_op jit(solution)/shard_map/all_gather | solution.py:95
  10.6 264.5 %reduce-scatter.9.cloned.1.call-start = ((), (), s32[]{:S(2)}) async-start(), calls=%async_computation.11 | async-start | bytes 3145728 | tf_op jit(solution)/shard_map/reduce_scatter | solution.py:49
  244.4 306.9 %all-gather.23.cloned.1.call-start = ((), (), s32[]{:S(2)}) async-start(), calls=%async_computation.12 | async-start | bytes 1572864 | tf_op jit(solution)/shard_map/all_gather | solution.py:45
  278.7 285.3 %all-gather.25.cloned.1.call-start = ((), (), s32[]{:S(2)}) async-start(), calls=%async_computation.13 | async-start | bytes 17825792 | tf_op jit(solution)/shard_map/all_gather | solution.py:132
  279.5 359.9 %all-gather.27.cloned.1.call-start = ((), (), s32[]{:S(2)}) async-start(), calls=%async_computation.14 | async-start | bytes 17825792 | tf_op jit(solution)/shard_map/all_gather | solution.py:133
  280.2 401.8 %reduce-scatter.11.cloned.1.call-start = ((), (), s32[]{:S(2)}) async-start(), calls=%async_computation.15 | async-start | bytes 3145728 | tf_op jit(solution)/shard_map/reduce_scatter | solution.py:49
  280.2 17.2 collective-permute-start
  297.4 17.0 collective-permute-start.1
  297.4 33.1 %collective-permute-start.8 = (bf16[128,4096]{1,0:T(8,128)(2,1)}, bf16[128,4096]{1,0:T(8,128)(2,1)S(1)}, u32[]{:S(2)}, u32[]{:S(2)}) collective-permute-start(bf16[128,4096]{1,0:T(8,128)(2,1)} %param.20), channel_id=1, source_target_pairs={{2,0},{4,2},{6,4},{8,6},{10,8},{12,10},{14,12},{16,14},{18,16},{20... | collective-permute-start | bytes 3145736 | tf_op jit(solution)/shard_map/ppermute | solution.py:30
  314.5 39.5 %collective-permute-start.2 = (bf16[128,4096]{1,0:T(8,128)(2,1)S(1)}, bf16[128,4096]{1,0:T(8,128)(2,1)S(1)}, u32[]{:S(2)}, u32[]{:S(2)}) collective-permute-start(bf16[128,4096]{1,0:T(8,128)(2,1)S(1)} %collective-permute-done.1), channel_id=1, source_target_pairs={{0,2},{2,4},{4,6},{6,8},{8,10},{10,12},{12,14},{14,16},{16,18},{18... | collective-permute-start | bytes 3145736 | tf_op jit(solution)/shard_map/ppermute | solution.py:28
  331.5 28.0 %collective-permute-start.9 = (bf16[128,4096]{1,0:T(8,128)(2,1)S(1)}, bf16[128,4096]{1,0:T(8,128)(2,1)S(1)}, u32[]{:S(2)}, u32[]{:S(2)}) collective-permute-start(bf16[128,4096]{1,0:T(8,128)(2,1)S(1)} %collective-permute-done.8), channel_id=1, source_target_pairs={{2,0},{4,2},{6,4},{8,6},{10,8},{12,10},{14,12},{16,14},{18,16},{20... | collective-permute-start | bytes 3145736 | tf_op jit(solution)/shard_map/ppermute | solution.py:30
  354.0 22.0 collective-permute-start.3
  359.5 36.9 %collective-permute-start.10 = (bf16[128,4096]{1,0:T(8,128)(2,1)S(1)}, bf16[128,4096]{1,0:T(8,128)(2,1)S(1)}, u32[]{:S(2)}, u32[]{:S(2)}) collective-permute-start(bf16[128,4096]{1,0:T(8,128)(2,1)S(1)} %collective-permute-done.9), channel_id=1, source_target_pairs={{2,0},{4,2},{6,4},{8,6},{10,8},{12,10},{14,12},{16,14},{18,16},{20... | collective-permute-start | bytes 3145736 | tf_op jit(solution)/shard_map/ppermute | solution.py:30
  376.0 39.5 %collective-permute-start.4 = (bf16[128,4096]{1,0:T(8,128)(2,1)S(1)}, bf16[128,4096]{1,0:T(8,128)(2,1)S(1)}, u32[]{:S(2)}, u32[]{:S(2)}) collective-permute-start(bf16[128,4096]{1,0:T(8,128)(2,1)S(1)} %collective-permute-done.3), channel_id=1, source_target_pairs={{0,2},{2,4},{4,6},{6,8},{8,10},{10,12},{12,14},{14,16},{16,18},{18... | collective-permute-start | bytes 3145736 | tf_op jit(solution)/shard_map/ppermute | solution.py:28
  396.4 41.5 %collective-permute-start.11 = (bf16[128,4096]{1,0:T(8,128)(2,1)S(1)}, bf16[128,4096]{1,0:T(8,128)(2,1)S(1)}, u32[]{:S(2)}, u32[]{:S(2)}) collective-permute-start(bf16[128,4096]{1,0:T(8,128)(2,1)S(1)} %collective-permute-done.10), channel_id=1, source_target_pairs={{2,0},{4,2},{6,4},{8,6},{10,8},{12,10},{14,12},{16,14},{18,16},{20... | collective-permute-start | bytes 3145736 | tf_op jit(solution)/shard_map/ppermute | solution.py:30
  415.5 24.7 %collective-permute-start.5 = (bf16[128,4096]{1,0:T(8,128)(2,1)S(1)}, bf16[128,4096]{1,0:T(8,128)(2,1)S(1)}, u32[]{:S(2)}, u32[]{:S(2)}) collective-permute-start(bf16[128,4096]{1,0:T(8,128)(2,1)S(1)} %collective-permute-done.4), channel_id=1, source_target_pairs={{0,2},{2,4},{4,6},{6,8},{8,10},{10,12},{12,14},{14,16},{16,18},{18... | collective-permute-start | bytes 3145736 | tf_op jit(solution)/shard_map/ppermute | solution.py:28
  438.9 31.8 %collective-permute-start.12 = (bf16[128,4096]{1,0:T(8,128)(2,1)S(1)}, bf16[128,4096]{1,0:T(8,128)(2,1)}, u32[]{:S(2)}, u32[]{:S(2)}) collective-permute-start(bf16[128,4096]{1,0:T(8,128)(2,1)S(1)} %collective-permute-done.11), channel_id=1, source_target_pairs={{2,0},{4,2},{6,4},{8,6},{10,8},{12,10},{14,12},{16,14},{18,16},{20... | collective-permute-start | bytes 3145736 | tf_op jit(solution)/shard_map/ppermute | solution.py:30
  440.2 58.2 %collective-permute-start.6 = (bf16[128,4096]{1,0:T(8,128)(2,1)S(1)}, bf16[128,4096]{1,0:T(8,128)(2,1)}, u32[]{:S(2)}, u32[]{:S(2)}) collective-permute-start(bf16[128,4096]{1,0:T(8,128)(2,1)S(1)} %collective-permute-done.5), channel_id=1, source_target_pairs={{0,2},{2,4},{4,6},{6,8},{8,10},{10,12},{12,14},{14,16},{16,18},{18... | collective-permute-start | bytes 3145736 | tf_op jit(solution)/shard_map/ppermute | solution.py:28
  470.7 27.8 %collective-permute-start.13 = (bf16[128,4096]{1,0:T(8,128)(2,1)}, bf16[128,4096]{1,0:T(8,128)(2,1)}, u32[]{:S(2)}, u32[]{:S(2)}) collective-permute-start(bf16[128,4096]{1,0:T(8,128)(2,1)} %collective-permute-done.12), channel_id=1, source_target_pairs={{2,0},{4,2},{6,4},{8,6},{10,8},{12,10},{14,12},{16,14},{18,16},{20... | collective-permute-start | bytes 3145736 | tf_op jit(solution)/shard_map/ppermute | solution.py:30
  498.4 17.3 collective-permute-start.7
  498.5 38.4 %collective-permute-start.14 = (bf16[128,4096]{1,0:T(8,128)(2,1)}, bf16[128,4096]{1,0:T(8,128)(2,1)S(1)}, u32[]{:S(2)}, u32[]{:S(2)}) collective-permute-start(bf16[128,4096]{1,0:T(8,128)(2,1)} %collective-permute-done.13), channel_id=1, source_target_pairs={{2,0},{4,2},{6,4},{8,6},{10,8},{12,10},{14,12},{16,14},{18,16},{20... | collective-permute-start | bytes 3145736 | tf_op jit(solution)/shard_map/ppermute | solution.py:30
  651.7 57.0 %all-gather.29.cloned.1.call-start = ((), (), s32[]{:S(2)}) async-start(), calls=%async_computation.16 | async-start | bytes 1572864 | tf_op jit(solution)/shard_map/all_gather | solution.py:45
  687.3 149.9 %all-gather.31.cloned.1.call-start = ((), (), s32[]{:S(2)}) async-start(), calls=%async_computation.17 | async-start | bytes 17825792 | tf_op jit(solution)/shard_map/all_gather | solution.py:156
  687.8 205.0 %reduce-scatter.13.cloned.1.call-start = ((), (), s32[]{:S(2)}) async-start(), calls=%async_computation.18 | async-start | bytes 3145728 | tf_op jit(solution)/shard_map/reduce_scatter | solution.py:49
  862.6 56.8 %all-gather.33.cloned.1.call-start = ((), (), s32[]{:S(2)}) async-start(), calls=%async_computation.19 | async-start | bytes 1572864 | tf_op jit(solution)/shard_map/all_gather | solution.py:45
  897.9 204.4 %reduce-scatter.19.cloned.1.call-start = ((), (), s32[]{:S(2)}) async-start(), calls=%async_computation.22 | async-start | bytes 1081344
  965.6 166.7 %reduce-scatter.15.cloned.1.call-start = ((), (), s32[]{:S(2)}) async-start(), calls=%async_computation.20 | async-start | bytes 3145728 | tf_op jit(solution)/shard_map/reduce_scatter | solution.py:49
  1009.3 1364.6 %reduce-scatter.17.cloned.1.call-start = ((), (), s32[]{:S(2)}) async-start(), calls=%async_computation.21 | async-start | bytes 142606336 | tf_op jit(solution)/shard_map/reduce_scatter | solution.py:233
  (51 other events, 979.9 us)
Sparse Core Ops, SparseCore 0:
  9.5 24.2 all-gather.12
  36.0 50.3 all-gather.16
  88.6 48.9 all-gather.18
  139.6 48.8 all-gather.14
  190.6 48.8 all-gather.20
  244.6 30.4 reduce-scatter.8
  278.8 21.2 all-gather.22
  302.3 188.7 all-gather.24
  493.3 146.0 all-gather.26
  651.8 30.0 reduce-scatter.10
  687.4 21.2 all-gather.28
  710.7 126.4 all-gather.30
  862.7 30.0 reduce-scatter.12
  898.0 21.2 all-gather.32
  965.7 136.5 reduce-scatter.18
  1104.4 27.9 reduce-scatter.14
  1136.4 1237.4 reduce-scatter.16
